TPU v7x, 512 devices: a whole 4x4x16 slice. The times are simulated.
512 devices in a mesh: row: 32 (over y_lo, z), col: 16 (over y_hi, x, core).
Axes of the slice: x: 4, y: 4 (y_hi: 2, y_lo: 2; y = y_hi * 2 + y_lo), z: 16, core: 2. Of those that a mesh axis runs over, the one named last changes fastest.
Arguments:
- inputs: bfloat16 [128, 1024, 2048], P('row', 'col'), may hold values from -6 to 6
- output_gradient: bfloat16 [128, 1024, 256], P('row', 'col'), may hold values from -6 to 6
- weight: bfloat16 [3, 3, 2048, 256], P(None, None, 'row'), may hold values from -0.125 to 0.125
Outputs:
- grad_in: bfloat16 [128, 1024, 2048], P('row', 'col')
- grad_weight: float32 [3, 3, 2048, 256], P(None, None, 'row')
All inputs are finite; a program needn't handle non-finite values.
Results may differ from a plain program's by a relative error of at most 0.001.
Values may be sent and summed in bfloat16 or wider, within the bound.
A program may use at most 128 MiB of HBM per device.

v0:
```python
import functools
import math

import jax
import jax.numpy as jnp
from jax import lax
from jax.experimental import pallas as pl
from jax.experimental.pallas import tpu as pltpu
from jax.sharding import PartitionSpec as P

MESH = pl.DeviceIdType.MESH
STEP = 12
PAD = 16
DZ = (-1, 0, 1, 2)


def mod(a, n):
    return lax.rem(a + 4 * n, n)


def kernel(scale, x_ref, g_ref, w_ref, gi_ref, gw_ref, gall, gs, xg, xt, wg, part, ry, ssum, rz, qsum, rl, fin, gib,
           s_g, r_g, s_f, s_h, r_h, s_x, r_x, s_w, r_w, s_y, r_y, s_z, r_z, s_l, r_l, s_a, r_a, s_o, r_o, l_sem):
    row, col = lax.axis_index("row"), lax.axis_index("col")
    z, y_lo = lax.rem(row, 16), lax.div(row, 16)
    k, y_hi = lax.rem(col, 8), lax.div(col, 8)
    x, c = lax.div(k, 2), lax.rem(k, 2)
    y = 2 * y_hi + y_lo
    sgn = 1 - 2 * c

    def dev(xx, yy, zz, cc):
        return (lax.rem(yy, 2) * 16 + zz, lax.div(yy, 2) * 8 + 2 * xx + cc)

    def ring(dx, dc):
        xx, cc = mod(x + dx, 4), mod(c + dc, 2)
        return dev(xx, y, z, cc), 2 * xx + cc

    def block(dy, dz):
        yy, zz = mod(y + dy, 4), mod(z + sgn * dz, 16)
        return dev(x, yy, zz, c), yy, zz

    own_row = 4 * k + y
    quarter, turn = lax.rem(z, 4), lax.div(z, 4)
    line_k, line_y = lax.div(row, 4), lax.rem(row, 4)
    line_q, line_s = lax.div(col, 4), lax.rem(col, 4)

    def line(m):
        return dev(lax.div(line_k, 2), line_y, 4 * m + line_q, lax.rem(line_k, 2))

    def same(d):
        return jnp.logical_and(d[0] == row, d[1] == col)

    barrier = pltpu.get_barrier_semaphore()

    def greet(d):
        pl.semaphore_signal(barrier, inc=1, device_id=d, device_id_type=MESH)

    for n in range(1, 16):
        greet((row, mod(col + n, 16)))
    for dy in range(4):
        for dz in DZ:
            if (dy, dz) != (0, 0):
                greet(block(-dy, -dz)[0])
    greet((mod(row + 3, 32), col))
    greet((mod(row - 3, 32), col))
    greet((own_row, 4 * quarter + turn))
    for m in range(4):
        greet(line(m))
    pl.semaphore_wait(barrier, 15 + 15 + 2 + 1 + 4)

    sends = []

    def send(src, dst, ss, rs, d):
        cp = pltpu.make_async_remote_copy(src_ref=src, dst_ref=dst, send_sem=ss, recv_sem=rs, device_id=d, device_id_type=MESH)
        cp.start()
        sends.append(cp)

    def arrived(dst, rs):
        pltpu.make_async_remote_copy(src_ref=dst, dst_ref=dst, send_sem=rs, recv_sem=rs, device_id=ring(0, 1)[0], device_id_type=MESH).wait_recv()

    def gpiece(t, kk):
        return gall.at[t, :, pl.ds(pl.multiple_of(PAD + 64 * kk, 16), 64), :]

    def xpiece(ref, kk):
        return ref.at[:, pl.ds(pl.multiple_of(64 * kk, 64), 64), :]

    def chans(ref, kk):
        return ref.at[:, :, pl.ds(pl.multiple_of(256 * kk, 256), 256)]

    def wpiece(i, p):
        return wg.at[:, pl.ds(pl.multiple_of(64 * i + 16 * p, 16), 16), :]

    send(g_ref, gpiece(0, k), s_g.at[0, 0], r_g.at[0, 0, 0], (mod(row + 3, 32), col))
    send(g_ref, gpiece(2, k), s_g.at[2, 0], r_g.at[2, 0, 0], (mod(row - 3, 32), col))
    own_g = pltpu.make_async_copy(g_ref, gpiece(1, k), r_g.at[1, 0, 0])
    own_g.start()
    w_to = (line(line_s), line_y, line_q)
    w_src = w_ref.at[:, pl.ds(pl.multiple_of(16 * line_q, 16), 16), :]
    w_self = same(w_to[0])
    w_remote = pltpu.make_async_remote_copy(src_ref=w_src, dst_ref=wpiece(line_y, line_q), send_sem=s_w.at[0, 1], recv_sem=r_w.at[0, 1], device_id=w_to[0], device_id_type=MESH)

    @pl.when(jnp.logical_not(w_self))
    def _():
        w_remote.start()

    @pl.when(w_self)
    def _():
        pltpu.make_async_copy(w_src, wpiece(line_y, line_q), r_w.at[0, 1]).start()

    is_edge = jnp.logical_or(jnp.logical_and(y_hi == 1, k == 0), jnp.logical_and(y_hi == 0, k == 7))
    edge_from = jnp.where(y_hi == 1, 0, 48)
    edge_to = jnp.where(y_hi == 1, PAD + 512, 0)
    other = 1 - y_hi

    def strip_copy(t, kk):
        src = gall.at[t, :, pl.ds(pl.multiple_of(PAD + 64 * k + edge_from, 16), 16), :]
        dst = gall.at[t, :, pl.ds(pl.multiple_of(edge_to, 16), 16), :]
        return pltpu.make_async_remote_copy(src_ref=src, dst_ref=dst, send_sem=s_h.at[t, kk], recv_sem=r_h.at[t], device_id=(row, 8 * other + kk), device_id_type=MESH)

    def spread(t):
        src = gpiece(t, k)
        for dx in (1, 3, 2):
            send(src, gpiece(t, k), s_f.at[t, dx], r_g.at[t, dx, 0], ring(dx, 0)[0])
        send(src, gpiece(t, k), s_f.at[t, 0], r_g.at[t, 0, 1], ring(0, 1)[0])

        @pl.when(is_edge)
        def _():
            for kk in range(8):
                strip_copy(t, kk).start()

    def hand_over(t):
        for dx in (1, 3, 2):
            kk = ring(-dx, 0)[1]
            arrived(gpiece(t, kk), r_g.at[t, dx, 0])
            send(gpiece(t, kk), gpiece(t, kk), s_g.at[t, dx], r_g.at[t, dx, 1], ring(0, 1)[0])

    own_g.wait()
    spread(1)
    for dx, dc in ((1, 0), (3, 0), (1, 1), (3, 1), (2, 0), (2, 1), (0, 1)):
        to, kk = ring(dx, dc)
        send(chans(x_ref, kk), xpiece(xg, k), s_x.at[dx, dc], r_x.at[dx, dc], to)
    own_x = pltpu.make_async_copy(chans(x_ref, k), xpiece(xg, k), r_x.at[0, 0])
    own_x.start()

    @pl.when(y_hi == 0)
    def _():
        gall[:, :, 0:PAD, :] = jnp.zeros((3, 4, PAD, 256), gall.dtype)

    @pl.when(y_hi == 1)
    def _():
        gall[:, :, PAD + 512 :, :] = jnp.zeros((3, 4, PAD, 256), gall.dtype)

    arrived(wpiece(y, quarter), r_w.at[0, 1])
    for dy in (1, 3, 2, 0):
        for dz in DZ:
            if (dy, dz) != (0, 0):
                send(wpiece(y, quarter), wpiece(y, quarter), s_w.at[dy, dz + 1], r_w2(r_w, dy, dz), block(dy, dz)[0])
    for t in (0, 2):
        arrived(gpiece(t, k), r_g.at[t, 0, 0])
        spread(t)
    hand_over(1)

    def tile_ready(t):
        for dx in range(4):
            arrived(gpiece(t, ring(-dx, 1)[1]), r_g.at[t, dx, 1])
        arrived(gall.at[t, :, pl.ds(pl.multiple_of(jnp.where(y_hi == 1, 0, PAD + 512), 16), 16), :], r_h.at[t])

    def shifts(t):
        valid = {0: row >= 3, 1: row >= 0, 2: row < 29}[t]

        def body(h, carry):
            for b in range(3):
                off = PAD + STEP * (1 - b)
                v = gall[t, h, off : off + 512, :]
                gs[t, b, pl.ds(pl.multiple_of(512 * h, 512), 512), :] = jnp.where(valid, v, jnp.zeros_like(v))
            return carry

        lax.fori_loop(0, 4, body, 0)

    def filter_terms(t):
        a = 2 - t

        def body(b, carry):
            part[a, b] = jnp.dot(xt[...], gs[t, b], preferred_element_type=jnp.float32)
            return carry

        lax.fori_loop(0, 3, body, 0)
        for dy in (1, 3, 2):
            to, yy, _ = block(dy, 0)
            send(part.at[a, :, pl.ds(pl.multiple_of(64 * yy, 64), 64), :], ry.at[a, dy - 1], s_y.at[a, dy], r_y.at[a, dy], to)

    own_x.wait()
    for dx, dc in ((1, 0), (3, 0), (1, 1), (3, 1), (2, 0), (2, 1), (0, 1)):
        arrived(xpiece(xg, ring(-dx, -dc)[1]), r_x.at[dx, dc])

    for h in range(4):
        xt[:, 512 * h : 512 * h + 512] = xg[h].T
    tile_ready(1)
    shifts(1)
    filter_terms(1)
    for t in (0, 2):
        hand_over(t)
    for t in (0, 2):
        tile_ready(t)
        shifts(t)
        filter_terms(t)

    for dy in (1, 3, 2, 0):
        for dz in DZ:
            if (dy, dz) != (0, 0):
                _, yy, zz = block(-dy, -dz)
                arrived(wpiece(yy, lax.rem(zz, 4)), r_w2(r_w, dy, dz))

    def back(h, carry):
        rows = pl.ds(pl.multiple_of(512 * h, 512), 512)
        total = jnp.zeros((512, 256), jnp.float32)
        for t in range(3):
            for b in range(3):
                total = total + lax.dot_general(
                    gs[t, b, rows, :], wg[3 * (2 - t) + b], (((1,), (1,)), ((), ())), preferred_element_type=jnp.float32
                )
        gib[h] = total.astype(gib.dtype)
        return carry

    lax.fori_loop(0, 4, back, 0)
    for dx, dc in ((1, 0), (3, 0), (1, 1), (3, 1), (2, 0), (2, 1), (0, 1)):
        to, kk = ring(dx, dc)
        send(xpiece(gib, kk), chans(gi_ref, k), s_o.at[dx, dc], r_o.at[dx, dc], to)
    own_o = pltpu.make_async_copy(xpiece(gib, k), chans(gi_ref, k), r_o.at[0, 0])
    own_o.start()

    for a in (1, 2, 0):
        for dy in (1, 3, 2):
            arrived(ry.at[a, dy - 1], r_y.at[a, dy])
        mine = part[a, :, pl.ds(pl.multiple_of(64 * y, 64), 64), :]
        ssum[a] = mine + ry[a, 0] + ry[a, 1] + ry[a, 2]
        for n, dz in enumerate((-1, 1, 2)):
            to, _, zz = block(0, dz)
            q = lax.rem(zz, 4)
            send(ssum.at[a, :, pl.ds(pl.multiple_of(16 * q, 16), 16), :], rz.at[a, n], s_z.at[a, n], r_z.at[a, n], to)
    for a in (1, 2, 0):
        for n in range(3):
            arrived(rz.at[a, n], r_z.at[a, n])
        mine = ssum[a, :, pl.ds(pl.multiple_of(16 * quarter, 16), 16), :]
        qsum[3 * a : 3 * a + 3] = mine + rz[a, 0] + rz[a, 1] + rz[a, 2]

    owners = []
    for s in range(4):
        to = (own_row, 4 * quarter + s)
        src = qsum.at[:, 8 * (s // 2) : 8 * (s // 2) + 8, 128 * (s % 2) : 128 * (s % 2) + 128]
        cp = pltpu.make_async_remote_copy(src_ref=src, dst_ref=rl.at[turn], send_sem=s_l.at[s], recv_sem=r_l.at[turn], device_id=to, device_id_type=MESH)
        me = same(to)

        @pl.when(jnp.logical_not(me))
        def _():
            cp.start()

        @pl.when(me)
        def _():
            pltpu.make_async_copy(src, rl.at[turn], r_l.at[turn]).start()

        owners.append((cp, me))
    for m in range(4):
        arrived(rl.at[m], r_l.at[m])
    fin[...] = (rl[0] + rl[1] + rl[2] + rl[3]) * scale

    def slot(cc):
        return gw_ref.at[
            :,
            pl.ds(pl.multiple_of(16 * lax.div(cc, 4) + 8 * lax.div(lax.rem(cc, 4), 2), 8), 8),
            pl.ds(pl.multiple_of(128 * lax.rem(cc, 2), 128), 128),
        ]

    for n in range(1, 16):
        send(fin, slot(col), s_a.at[n], r_a.at[n], (row, mod(col + n, 16)))
    own_f = pltpu.make_async_copy(fin, slot(col), l_sem)
    own_f.start()

    for dx, dc in ((1, 0), (3, 0), (1, 1), (3, 1), (2, 0), (2, 1), (0, 1)):
        arrived(chans(gi_ref, ring(-dx, -dc)[1]), r_o.at[dx, dc])
    own_o.wait()
    for n in range(1, 16):
        arrived(slot(mod(col - n, 16)), r_a.at[n])
    own_f.wait()
    for cp in sends:
        cp.wait_send()

    @pl.when(jnp.logical_not(w_self))
    def _():
        w_remote.wait_send()

    for cp, me in owners:

        @pl.when(jnp.logical_not(me))
        def _():
            cp.wait_send()

    @pl.when(is_edge)
    def _():
        for t in range(3):
            for kk in range(8):
                strip_copy(t, kk).wait_send()


def r_w2(r_w, dy, dz):
    return r_w.at[dy, dz + 1]


def shards(inputs, output_gradient, weight):
    height, width, in_chans = inputs.shape
    total = height * width * lax.axis_size("row") * lax.axis_size("col")
    bf, f32 = jnp.bfloat16, jnp.float32
    dma = pltpu.SemaphoreType.DMA
    scratch = [
        pltpu.VMEM((3, 4, 2 * PAD + 512, 256), bf),
        pltpu.VMEM((3, 3, 2048, 256), bf),
        pltpu.VMEM((4, 512, 256), bf),
        pltpu.VMEM((256, 2048), bf),
        pltpu.VMEM((9, 256, 256), bf),
        pltpu.VMEM((3, 3, 256, 256), f32),
        pltpu.VMEM((3, 3, 3, 64, 256), f32),
        pltpu.VMEM((3, 3, 64, 256), f32),
        pltpu.VMEM((3, 3, 3, 16, 256), f32),
        pltpu.VMEM((9, 16, 256), f32),
        pltpu.VMEM((4, 9, 8, 128), f32),
        pltpu.VMEM((9, 8, 128), f32),
        pltpu.VMEM((4, 512, 256), bf),
        dma((3, 4)), dma((3, 4, 2)), dma((3, 4)), dma((3, 8)), dma((3,)),
        dma((4, 2)), dma((4, 2)), dma((4, 4)), dma((4, 4)),
        dma((3, 4)), dma((3, 4)), dma((3, 3)), dma((3, 3)),
        dma((4,)), dma((4,)), dma((16,)), dma((16,)), dma((4, 2)), dma((4, 2)), dma,
    ]
    hbm = pl.BlockSpec(memory_space=pl.ANY)
    grad_in, grad_weight = pl.pallas_call(
        functools.partial(kernel, 1.0 / math.sqrt(total)),
        out_shape=(jax.ShapeDtypeStruct(inputs.shape, bf), jax.ShapeDtypeStruct((9,) + weight.shape[2:], f32)),
        in_specs=[hbm] * 3,
        out_specs=(hbm, hbm),
        scratch_shapes=scratch,
        compiler_params=pltpu.CompilerParams(collective_id=0, has_side_effects=True, vmem_limit_bytes=56 * 1024 * 1024),
    )(inputs, output_gradient, weight.reshape((9,) + weight.shape[2:]))
    return grad_in, grad_weight.reshape(weight.shape)


def solution(mesh):
    return jax.shard_map(
        shards,
        mesh=mesh,
        in_specs=(P("row", "col", None), P("row", "col", None), P(None, None, "row", None)),
        out_specs=(P("row", "col", None), P(None, None, "row", None)),
        check_vma=False,
    )
```

profile of v0, /device:TPU:97, one launch (start us, length us, event | category | flops | bytes accessed | tf_op | source)
XLA Modules:
  0.0 116.4 jit_solution(11706255510668627571)
XLA Ops:
  0.6 112.6 %shard_map.50 = (bf16[4,64,2048]{2,1,0:T(8,128)(2,1)}, f32[9,64,256]{2,1,0:T(8,128)}) custom-call(bf16[4,64,2048]{2,1,0:T(8,128)(2,1)} %x_ref.1, bf16[4,64,256]{2,1,0:T(8,128)(2,1)} %g_ref.1, bf16[9,64,256]{2,1,0:T(8,128)(2,1)} %bitcast.3), custom_call_target="tpu_custom_call" | custom-call | tf_op jit(solution)/shard_map/pallas_call | solution.py:333
  113.2 0.0 copy-start
  113.2 2.4 %copy.7 = bf16[4,64,2048]{2,1,0:T(8,128)(2,1)} copy(bf16[4,64,2048]{2,1,0:T(8,128)(2,1)} %get-tuple-element.8) | data formatting | bytes 2097152
  115.6 0.0 copy-done
  115.6 0.8 copy.8
Async XLA Ops:
  113.2 2.4 %copy-start = (f32[9,64,256]{2,1,0:T(8,128)S(1)}, f32[9,64,256]{2,1,0:T(8,128)}, u32[]{:S(2)}) copy-start(f32[9,64,256]{2,1,0:T(8,128)} %get-tuple-element.5) | copy-start | bytes 1769476
where the time goes:
time: 117 us; the launch traced here: 116 us
  Pallas kernels  113 us (97%)
  local copies, waits for them, and re-layouts  3.18 us (3%)
    pallas_call x1, Pallas kernels, shards(): pl.pallas_call(functools.partial(kernel, 1.0 / math.sqrt(total)), out_sha...  113 us
    unnamed x4, local copies, waits for them, and re-layouts  3.18 us

commit v1 on v0

--- a/solution.py
+++ b/solution.py
@@ -18,8 +18,8 @@
     return lax.rem(a + 4 * n, n)
 
 
-def kernel(scale, x_ref, g_ref, w_ref, gi_ref, gw_ref, gall, gs, xg, xt, wg, part, ry, ssum, rz, qsum, rl, fin, gib,
-           s_g, r_g, s_f, s_h, r_h, s_x, r_x, s_w, r_w, s_y, r_y, s_z, r_z, s_l, r_l, s_a, r_a, s_o, r_o, l_sem):
+def kernel(scale, x_ref, g_ref, w_ref, gi_ref, gw_ref, gall, gs, xg, xt, wg, part, ry, rz, suma, sumb, rz2, ry2, qsum, rl, rm, fin, gib,
+           s_g, r_g, s_f, s_h, r_h, s_x, r_x, s_w, r_w, s_y, r_y, s_z, r_z, s_y2, r_y2, s_z2, r_z2, s_l, r_l, s_m, r_m, s_a, r_a, s_o, r_o, l_sem):
     row, col = lax.axis_index("row"), lax.axis_index("col")
     z, y_lo = lax.rem(row, 16), lax.div(row, 16)
     k, y_hi = lax.rem(col, 8), lax.div(col, 8)
@@ -38,13 +38,19 @@
         yy, zz = mod(y + dy, 4), mod(z + sgn * dz, 16)
         return dev(x, yy, zz, c), yy, zz
 
-    own_row = 4 * k + y
     quarter, turn = lax.rem(z, 4), lax.div(z, 4)
     line_k, line_y = lax.div(row, 4), lax.rem(row, 4)
     line_q, line_s = lax.div(col, 4), lax.rem(col, 4)
 
     def line(m):
         return dev(lax.div(line_k, 2), line_y, 4 * m + line_q, lax.rem(line_k, 2))
+
+    def holder(m):
+        kk = 4 * y_lo + m
+        return dev(lax.div(kk, 2), lax.div(col, 4), z, lax.rem(kk, 2))
+
+    def along(n):
+        return dev(x, y, mod(z + 4 * n, 16), c)
 
     def same(d):
         return jnp.logical_and(d[0] == row, d[1] == col)
@@ -62,10 +68,12 @@
                 greet(block(-dy, -dz)[0])
     greet((mod(row + 3, 32), col))
     greet((mod(row - 3, 32), col))
-    greet((own_row, 4 * quarter + turn))
+    greet((4 * k + y, 4 * quarter + turn))
     for m in range(4):
-        greet(line(m))
-    pl.semaphore_wait(barrier, 15 + 15 + 2 + 1 + 4)
+        greet(holder(m))
+    for n in range(1, 4):
+        greet(along(-n))
+    pl.semaphore_wait(barrier, 15 + 15 + 2 + 1 + 4 + 3)
 
     sends = []
 
@@ -112,12 +120,15 @@
     other = 1 - y_hi
 
     def strip_copy(t, kk):
-        src = gall.at[t, :, pl.ds(pl.multiple_of(PAD + 64 * k + edge_from, 16), 16), :]
+        if t == 1:
+            src = g_ref.at[:, pl.ds(pl.multiple_of(edge_from, 16), 16), :]
+        else:
+            src = gall.at[t, :, pl.ds(pl.multiple_of(PAD + 64 * k + edge_from, 16), 16), :]
         dst = gall.at[t, :, pl.ds(pl.multiple_of(edge_to, 16), 16), :]
         return pltpu.make_async_remote_copy(src_ref=src, dst_ref=dst, send_sem=s_h.at[t, kk], recv_sem=r_h.at[t], device_id=(row, 8 * other + kk), device_id_type=MESH)
 
     def spread(t):
-        src = gpiece(t, k)
+        src = g_ref if t == 1 else gpiece(t, k)
         for dx in (1, 3, 2):
             send(src, gpiece(t, k), s_f.at[t, dx], r_g.at[t, dx, 0], ring(dx, 0)[0])
         send(src, gpiece(t, k), s_f.at[t, 0], r_g.at[t, 0, 1], ring(0, 1)[0])
@@ -133,7 +144,6 @@
             arrived(gpiece(t, kk), r_g.at[t, dx, 0])
             send(gpiece(t, kk), gpiece(t, kk), s_g.at[t, dx], r_g.at[t, dx, 1], ring(0, 1)[0])
 
-    own_g.wait()
     spread(1)
     for dx, dc in ((1, 0), (3, 0), (1, 1), (3, 1), (2, 0), (2, 1), (0, 1)):
         to, kk = ring(dx, dc)
@@ -154,10 +164,11 @@
         for dz in DZ:
             if (dy, dz) != (0, 0):
                 send(wpiece(y, quarter), wpiece(y, quarter), s_w.at[dy, dz + 1], r_w2(r_w, dy, dz), block(dy, dz)[0])
+    hand_over(1)
     for t in (0, 2):
         arrived(gpiece(t, k), r_g.at[t, 0, 0])
         spread(t)
-    hand_over(1)
+    own_g.wait()
 
     def tile_ready(t):
         for dx in range(4):
@@ -180,13 +191,38 @@
         a = 2 - t
 
         def body(b, carry):
-            part[a, b] = jnp.dot(xt[...], gs[t, b], preferred_element_type=jnp.float32)
+            part[a, b] = jnp.dot(xt[...], gs[t, b], preferred_element_type=jnp.float32).reshape(4, 4, 16, 256)
             return carry
 
         lax.fori_loop(0, 3, body, 0)
         for dy in (1, 3, 2):
             to, yy, _ = block(dy, 0)
-            send(part.at[a, :, pl.ds(pl.multiple_of(64 * yy, 64), 64), :], ry.at[a, dy - 1], s_y.at[a, dy], r_y.at[a, dy], to)
+            send(part.at[a, :, :, yy, :, 0:128], ry.at[a, dy - 1], s_y.at[a, dy], r_y.at[a, dy], to)
+        for n, dz in enumerate((-1, 1, 2)):
+            to, _, zz = block(0, dz)
+            send(part.at[a, :, lax.rem(zz, 4), :, :, 128:256], rz.at[a, n], s_z.at[a, n], r_z.at[a, n], to)
+
+    def first_sums(a):
+        for dy in (1, 3, 2):
+            arrived(ry.at[a, dy - 1], r_y.at[a, dy])
+        suma[a] = part[a, :, :, y, :, 0:128] + ry[a, 0] + ry[a, 1] + ry[a, 2]
+        for n, dz in enumerate((-1, 1, 2)):
+            to, _, zz = block(0, dz)
+            send(suma.at[a, :, lax.rem(zz, 4)], rz2.at[a, n], s_z2.at[a, n], r_z2.at[a, n], to)
+        for n in range(3):
+            arrived(rz.at[a, n], r_z.at[a, n])
+        sumb[a] = part[a, :, quarter, :, :, 128:256] + rz[a, 0] + rz[a, 1] + rz[a, 2]
+        for dy in (1, 3, 2):
+            to, yy, _ = block(dy, 0)
+            send(sumb.at[a, :, yy], ry2.at[a, dy - 1], s_y2.at[a, dy], r_y2.at[a, dy], to)
+
+    def second_sums(a):
+        for n in range(3):
+            arrived(rz2.at[a, n], r_z2.at[a, n])
+        qsum[3 * a : 3 * a + 3, :, 0:128] = suma[a, :, quarter] + rz2[a, 0] + rz2[a, 1] + rz2[a, 2]
+        for dy in (1, 3, 2):
+            arrived(ry2.at[a, dy - 1], r_y2.at[a, dy])
+        qsum[3 * a : 3 * a + 3, :, 128:256] = sumb[a, :, y] + ry2[a, 0] + ry2[a, 1] + ry2[a, 2]
 
     own_x.wait()
     for dx, dc in ((1, 0), (3, 0), (1, 1), (3, 1), (2, 0), (2, 1), (0, 1)):
@@ -199,10 +235,13 @@
     filter_terms(1)
     for t in (0, 2):
         hand_over(t)
-    for t in (0, 2):
-        tile_ready(t)
-        shifts(t)
-        filter_terms(t)
+    tile_ready(0)
+    shifts(0)
+    filter_terms(0)
+    first_sums(1)
+    tile_ready(2)
+    shifts(2)
+    filter_terms(2)
 
     for dy in (1, 3, 2, 0):
         for dz in DZ:
@@ -228,26 +267,18 @@
     own_o = pltpu.make_async_copy(xpiece(gib, k), chans(gi_ref, k), r_o.at[0, 0])
     own_o.start()
 
-    for a in (1, 2, 0):
-        for dy in (1, 3, 2):
-            arrived(ry.at[a, dy - 1], r_y.at[a, dy])
-        mine = part[a, :, pl.ds(pl.multiple_of(64 * y, 64), 64), :]
-        ssum[a] = mine + ry[a, 0] + ry[a, 1] + ry[a, 2]
-        for n, dz in enumerate((-1, 1, 2)):
-            to, _, zz = block(0, dz)
-            q = lax.rem(zz, 4)
-            send(ssum.at[a, :, pl.ds(pl.multiple_of(16 * q, 16), 16), :], rz.at[a, n], s_z.at[a, n], r_z.at[a, n], to)
-    for a in (1, 2, 0):
-        for n in range(3):
-            arrived(rz.at[a, n], r_z.at[a, n])
-        mine = ssum[a, :, pl.ds(pl.multiple_of(16 * quarter, 16), 16), :]
-        qsum[3 * a : 3 * a + 3] = mine + rz[a, 0] + rz[a, 1] + rz[a, 2]
-
-    owners = []
+    first_sums(2)
+    second_sums(1)
+    first_sums(0)
+    second_sums(2)
+    second_sums(0)
+
+    passed = []
     for s in range(4):
-        to = (own_row, 4 * quarter + s)
+        to = (16 * lax.div(k, 4) + z, 4 * y + s)
+        slot_k = lax.rem(k, 4)
         src = qsum.at[:, 8 * (s // 2) : 8 * (s // 2) + 8, 128 * (s % 2) : 128 * (s % 2) + 128]
-        cp = pltpu.make_async_remote_copy(src_ref=src, dst_ref=rl.at[turn], send_sem=s_l.at[s], recv_sem=r_l.at[turn], device_id=to, device_id_type=MESH)
+        cp = pltpu.make_async_remote_copy(src_ref=src, dst_ref=rl.at[slot_k], send_sem=s_l.at[s], recv_sem=r_l.at[slot_k], device_id=to, device_id_type=MESH)
         me = same(to)
 
         @pl.when(jnp.logical_not(me))
@@ -256,12 +287,16 @@
 
         @pl.when(me)
         def _():
-            pltpu.make_async_copy(src, rl.at[turn], r_l.at[turn]).start()
-
-        owners.append((cp, me))
+            pltpu.make_async_copy(src, rl.at[slot_k], r_l.at[slot_k]).start()
+
+        passed.append((cp, me))
     for m in range(4):
         arrived(rl.at[m], r_l.at[m])
-    fin[...] = (rl[0] + rl[1] + rl[2] + rl[3]) * scale
+    for n in range(1, 4):
+        send(rl.at[lax.rem(turn + n, 4)], rm.at[n - 1], s_m.at[n], r_m.at[n], along(n))
+    for n in range(1, 4):
+        arrived(rm.at[n - 1], r_m.at[n])
+    fin[...] = (rl[turn] + rm[0] + rm[1] + rm[2]) * scale
 
     def slot(cc):
         return gw_ref.at[
@@ -288,7 +323,7 @@
     def _():
         w_remote.wait_send()
 
-    for cp, me in owners:
+    for cp, me in passed:
 
         @pl.when(jnp.logical_not(me))
         def _():
@@ -316,18 +351,22 @@
         pltpu.VMEM((4, 512, 256), bf),
         pltpu.VMEM((256, 2048), bf),
         pltpu.VMEM((9, 256, 256), bf),
-        pltpu.VMEM((3, 3, 256, 256), f32),
-        pltpu.VMEM((3, 3, 3, 64, 256), f32),
-        pltpu.VMEM((3, 3, 64, 256), f32),
-        pltpu.VMEM((3, 3, 3, 16, 256), f32),
+        pltpu.VMEM((3, 3, 4, 4, 16, 256), f32),
+        pltpu.VMEM((3, 3, 3, 4, 16, 128), f32),
+        pltpu.VMEM((3, 3, 3, 4, 16, 128), f32),
+        pltpu.VMEM((3, 3, 4, 16, 128), f32),
+        pltpu.VMEM((3, 3, 4, 16, 128), f32),
+        pltpu.VMEM((3, 3, 3, 16, 128), f32),
+        pltpu.VMEM((3, 3, 3, 16, 128), f32),
         pltpu.VMEM((9, 16, 256), f32),
         pltpu.VMEM((4, 9, 8, 128), f32),
+        pltpu.VMEM((3, 9, 8, 128), f32),
         pltpu.VMEM((9, 8, 128), f32),
         pltpu.VMEM((4, 512, 256), bf),
         dma((3, 4)), dma((3, 4, 2)), dma((3, 4)), dma((3, 8)), dma((3,)),
         dma((4, 2)), dma((4, 2)), dma((4, 4)), dma((4, 4)),
-        dma((3, 4)), dma((3, 4)), dma((3, 3)), dma((3, 3)),
-        dma((4,)), dma((4,)), dma((16,)), dma((16,)), dma((4, 2)), dma((4, 2)), dma,
+        dma((3, 4)), dma((3, 4)), dma((3, 3)), dma((3, 3)), dma((3, 4)), dma((3, 4)), dma((3, 3)), dma((3, 3)),
+        dma((4,)), dma((4,)), dma((4,)), dma((4,)), dma((16,)), dma((16,)), dma((4, 2)), dma((4, 2)), dma,
     ]
     hbm = pl.BlockSpec(memory_space=pl.ANY)
     grad_in, grad_weight = pl.pallas_call(

time: 117 us -> 103 us (0.88)
  the two profiles are of different devices: /device:TPU:97 before, /device:TPU:33 now
where the time goes in v1:
time: 103 us
  Pallas kernels  99 us (96%)
  local copies, waits for them, and re-layouts  3.18 us (3%)
    pallas_call x1, Pallas kernels, shards(): pl.pallas_call(functools.partial(kernel, 1.0 / math.sqrt(total)), out_sha...  99 us
    unnamed x4, local copies, waits for them, and re-layouts  3.18 us

profile of v1, /device:TPU:33, one launch (start us, length us, event | category | flops | bytes accessed | tf_op | source)
XLA Modules:
  0.0 102.9 jit_solution(8389810606986752713)
XLA Ops:
  0.6 99.0 %shard_map.50 = (bf16[4,64,2048]{2,1,0:T(8,128)(2,1)}, f32[9,64,256]{2,1,0:T(8,128)}) custom-call(bf16[4,64,2048]{2,1,0:T(8,128)(2,1)} %x_ref.1, bf16[4,64,256]{2,1,0:T(8,128)(2,1)} %g_ref.1, bf16[9,64,256]{2,1,0:T(8,128)(2,1)} %bitcast.3), custom_call_target="tpu_custom_call" | custom-call | tf_op jit(solution)/shard_map/pallas_call | solution.py:372
  99.7 0.0 copy-start
  99.7 2.4 %copy.7 = bf16[4,64,2048]{2,1,0:T(8,128)(2,1)} copy(bf16[4,64,2048]{2,1,0:T(8,128)(2,1)} %get-tuple-element.8) | data formatting | bytes 2097152
  102.1 0.0 copy-done
  102.1 0.8 copy.8
Async XLA Ops:
  99.7 2.4 %copy-start = (f32[9,64,256]{2,1,0:T(8,128)S(1)}, f32[9,64,256]{2,1,0:T(8,128)}, u32[]{:S(2)}) copy-start(f32[9,64,256]{2,1,0:T(8,128)} %get-tuple-element.5) | copy-start | bytes 1769476

commit v2 on v1

--- a/solution.py
+++ b/solution.py
@@ -18,8 +18,8 @@
     return lax.rem(a + 4 * n, n)
 
 
-def kernel(scale, x_ref, g_ref, w_ref, gi_ref, gw_ref, gall, gs, xg, xt, wg, part, ry, rz, suma, sumb, rz2, ry2, qsum, rl, rm, fin, gib,
-           s_g, r_g, s_f, s_h, r_h, s_x, r_x, s_w, r_w, s_y, r_y, s_z, r_z, s_y2, r_y2, s_z2, r_z2, s_l, r_l, s_m, r_m, s_a, r_a, s_o, r_o, l_sem):
+def kernel(scale, x_ref, g_ref, w_ref, gi_ref, gw_ref, gall, gs, xg, xt, wg, part, ry, rz, suma, sumb, rz2, ry2, qsum, rl, fin, gib,
+           s_g, r_g, s_f, s_h, r_h, s_x, r_x, s_w, r_w, s_y, r_y, s_z, r_z, s_y2, r_y2, s_z2, r_z2, s_l, r_l, s_a, r_a, s_o, r_o, l_sem):
     row, col = lax.axis_index("row"), lax.axis_index("col")
     z, y_lo = lax.rem(row, 16), lax.div(row, 16)
     k, y_hi = lax.rem(col, 8), lax.div(col, 8)
@@ -46,11 +46,8 @@
         return dev(lax.div(line_k, 2), line_y, 4 * m + line_q, lax.rem(line_k, 2))
 
     def holder(m):
-        kk = 4 * y_lo + m
-        return dev(lax.div(kk, 2), lax.div(col, 4), z, lax.rem(kk, 2))
-
-    def along(n):
-        return dev(x, y, mod(z + 4 * n, 16), c)
+        kk = lax.div(row, 4)
+        return dev(lax.div(kk, 2), lax.div(col, 4), 4 * m + quarter, lax.rem(kk, 2))
 
     def same(d):
         return jnp.logical_and(d[0] == row, d[1] == col)
@@ -71,9 +68,7 @@
     greet((4 * k + y, 4 * quarter + turn))
     for m in range(4):
         greet(holder(m))
-    for n in range(1, 4):
-        greet(along(-n))
-    pl.semaphore_wait(barrier, 15 + 15 + 2 + 1 + 4 + 3)
+    pl.semaphore_wait(barrier, 15 + 15 + 2 + 1 + 4)
 
     sends = []
 
@@ -219,10 +214,29 @@
     def second_sums(a):
         for n in range(3):
             arrived(rz2.at[a, n], r_z2.at[a, n])
-        qsum[3 * a : 3 * a + 3, :, 0:128] = suma[a, :, quarter] + rz2[a, 0] + rz2[a, 1] + rz2[a, 2]
+        qsum[a, :, :, 0:128] = suma[a, :, quarter] + rz2[a, 0] + rz2[a, 1] + rz2[a, 2]
         for dy in (1, 3, 2):
             arrived(ry2.at[a, dy - 1], r_y2.at[a, dy])
-        qsum[3 * a : 3 * a + 3, :, 128:256] = sumb[a, :, y] + ry2[a, 0] + ry2[a, 1] + ry2[a, 2]
+        qsum[a, :, :, 128:256] = sumb[a, :, y] + ry2[a, 0] + ry2[a, 1] + ry2[a, 2]
+
+    passed = []
+
+    def to_owner(a):
+        for s in range(4):
+            to = (4 * k + quarter, 4 * y + s)
+            src = qsum.at[a, :, 8 * (s // 2) : 8 * (s // 2) + 8, 128 * (s % 2) : 128 * (s % 2) + 128]
+            cp = pltpu.make_async_remote_copy(src_ref=src, dst_ref=rl.at[a, turn], send_sem=s_l.at[a, s], recv_sem=r_l.at[a, turn], device_id=to, device_id_type=MESH)
+            me = same(to)
+
+            @pl.when(jnp.logical_not(me))
+            def _():
+                cp.start()
+
+            @pl.when(me)
+            def _():
+                pltpu.make_async_copy(src, rl.at[a, turn], r_l.at[a, turn]).start()
+
+            passed.append((cp, me))
 
     own_x.wait()
     for dx, dc in ((1, 0), (3, 0), (1, 1), (3, 1), (2, 0), (2, 1), (0, 1)):
@@ -242,6 +256,9 @@
     tile_ready(2)
     shifts(2)
     filter_terms(2)
+    second_sums(1)
+    to_owner(1)
+    first_sums(2)
 
     for dy in (1, 3, 2, 0):
         for dz in DZ:
@@ -267,36 +284,16 @@
     own_o = pltpu.make_async_copy(xpiece(gib, k), chans(gi_ref, k), r_o.at[0, 0])
     own_o.start()
 
-    first_sums(2)
-    second_sums(1)
     first_sums(0)
     second_sums(2)
+    to_owner(2)
     second_sums(0)
-
-    passed = []
-    for s in range(4):
-        to = (16 * lax.div(k, 4) + z, 4 * y + s)
-        slot_k = lax.rem(k, 4)
-        src = qsum.at[:, 8 * (s // 2) : 8 * (s // 2) + 8, 128 * (s % 2) : 128 * (s % 2) + 128]
-        cp = pltpu.make_async_remote_copy(src_ref=src, dst_ref=rl.at[slot_k], send_sem=s_l.at[s], recv_sem=r_l.at[slot_k], device_id=to, device_id_type=MESH)
-        me = same(to)
-
-        @pl.when(jnp.logical_not(me))
-        def _():
-            cp.start()
-
-        @pl.when(me)
-        def _():
-            pltpu.make_async_copy(src, rl.at[slot_k], r_l.at[slot_k]).start()
-
-        passed.append((cp, me))
-    for m in range(4):
-        arrived(rl.at[m], r_l.at[m])
-    for n in range(1, 4):
-        send(rl.at[lax.rem(turn + n, 4)], rm.at[n - 1], s_m.at[n], r_m.at[n], along(n))
-    for n in range(1, 4):
-        arrived(rm.at[n - 1], r_m.at[n])
-    fin[...] = (rl[turn] + rm[0] + rm[1] + rm[2]) * scale
+    to_owner(0)
+
+    for a in (1, 2, 0):
+        for m in range(4):
+            arrived(rl.at[a, m], r_l.at[a, m])
+        fin[3 * a : 3 * a + 3] = (rl[a, 0] + rl[a, 1] + rl[a, 2] + rl[a, 3]) * scale
 
     def slot(cc):
         return gw_ref.at[
@@ -358,15 +355,14 @@
         pltpu.VMEM((3, 3, 4, 16, 128), f32),
         pltpu.VMEM((3, 3, 3, 16, 128), f32),
         pltpu.VMEM((3, 3, 3, 16, 128), f32),
-        pltpu.VMEM((9, 16, 256), f32),
-        pltpu.VMEM((4, 9, 8, 128), f32),
-        pltpu.VMEM((3, 9, 8, 128), f32),
+        pltpu.VMEM((3, 3, 16, 256), f32),
+        pltpu.VMEM((3, 4, 3, 8, 128), f32),
         pltpu.VMEM((9, 8, 128), f32),
         pltpu.VMEM((4, 512, 256), bf),
         dma((3, 4)), dma((3, 4, 2)), dma((3, 4)), dma((3, 8)), dma((3,)),
         dma((4, 2)), dma((4, 2)), dma((4, 4)), dma((4, 4)),
         dma((3, 4)), dma((3, 4)), dma((3, 3)), dma((3, 3)), dma((3, 4)), dma((3, 4)), dma((3, 3)), dma((3, 3)),
-        dma((4,)), dma((4,)), dma((4,)), dma((4,)), dma((16,)), dma((16,)), dma((4, 2)), dma((4, 2)), dma,
+        dma((3, 4)), dma((3, 4)), dma((16,)), dma((16,)), dma((4, 2)), dma((4, 2)), dma,
     ]
     hbm = pl.BlockSpec(memory_space=pl.ANY)
     grad_in, grad_weight = pl.pallas_call(

time: 103 us -> 99.1 us (0.962)
  the two profiles are of different devices: /device:TPU:33 before, /device:TPU:13 now
where the time goes in v2:
time: 99.1 us; the launch traced here: 98.9 us
  Pallas kernels  95.1 us (96%)
  local copies, waits for them, and re-layouts  3.18 us (3%)
    pallas_call x1, Pallas kernels, shards(): pl.pallas_call(functools.partial(kernel, 1.0 / math.sqrt(total)), out_sha...  95.1 us
    unnamed x4, local copies, waits for them, and re-layouts  3.18 us

profile of v2, /device:TPU:13, one launch (start us, length us, event | category | flops | bytes accessed | tf_op | source)
XLA Modules:
  0.0 98.9 jit_solution(14212438209883597266)
XLA Ops:
  0.6 95.1 %shard_map.50 = (bf16[4,64,2048]{2,1,0:T(8,128)(2,1)}, f32[9,64,256]{2,1,0:T(8,128)}) custom-call(bf16[4,64,2048]{2,1,0:T(8,128)(2,1)} %x_ref.1, bf16[4,64,256]{2,1,0:T(8,128)(2,1)} %g_ref.1, bf16[9,64,256]{2,1,0:T(8,128)(2,1)} %bitcast.3), custom_call_target="tpu_custom_call" | custom-call | tf_op jit(solution)/shard_map/pallas_call | solution.py:368
  95.7 0.0 copy-start
  95.7 2.4 %copy.7 = bf16[4,64,2048]{2,1,0:T(8,128)(2,1)} copy(bf16[4,64,2048]{2,1,0:T(8,128)(2,1)} %get-tuple-element.8) | data formatting | bytes 2097152
  98.1 0.0 copy-done
  98.1 0.8 copy.8
Async XLA Ops:
  95.7 2.4 %copy-start = (f32[9,64,256]{2,1,0:T(8,128)S(1)}, f32[9,64,256]{2,1,0:T(8,128)}, u32[]{:S(2)}) copy-start(f32[9,64,256]{2,1,0:T(8,128)} %get-tuple-element.5) | copy-start | bytes 1769476

commit v3 on v2

--- a/solution.py
+++ b/solution.py
@@ -57,17 +57,17 @@
     def greet(d):
         pl.semaphore_signal(barrier, inc=1, device_id=d, device_id_type=MESH)
 
-    for n in range(1, 16):
-        greet((row, mod(col + n, 16)))
+    greet((4 * k + y, 4 * quarter + turn))
+    for m in range(4):
+        greet(holder(m))
+    greet((mod(row + 3, 32), col))
+    greet((mod(row - 3, 32), col))
     for dy in range(4):
         for dz in DZ:
             if (dy, dz) != (0, 0):
                 greet(block(-dy, -dz)[0])
-    greet((mod(row + 3, 32), col))
-    greet((mod(row - 3, 32), col))
-    greet((4 * k + y, 4 * quarter + turn))
-    for m in range(4):
-        greet(holder(m))
+    for n in range(1, 16):
+        greet((row, mod(col + n, 16)))
     pl.semaphore_wait(barrier, 15 + 15 + 2 + 1 + 4)
 
     sends = []

time: 99.1 us -> 99.3 us (level)
  the two profiles are of different devices: /device:TPU:13 before, /device:TPU:5 now
where the time goes in v3:
time: 99.3 us; the launch traced here: 99.2 us
  Pallas kernels  95.3 us (96%)
  local copies, waits for them, and re-layouts  3.18 us (3%)
    pallas_call x1, Pallas kernels, shards(): pl.pallas_call(functools.partial(kernel, 1.0 / math.sqrt(total)), out_sha...  95.3 us
    unnamed x4, local copies, waits for them, and re-layouts  3.18 us

profile of v3, /device:TPU:5, one launch (start us, length us, event | category | flops | bytes accessed | tf_op | source)
XLA Modules:
  0.0 99.2 jit_solution(1882790922551143863)
XLA Ops:
  0.6 95.3 %shard_map.50 = (bf16[4,64,2048]{2,1,0:T(8,128)(2,1)}, f32[9,64,256]{2,1,0:T(8,128)}) custom-call(bf16[4,64,2048]{2,1,0:T(8,128)(2,1)} %x_ref.1, bf16[4,64,256]{2,1,0:T(8,128)(2,1)} %g_ref.1, bf16[9,64,256]{2,1,0:T(8,128)(2,1)} %bitcast.3), custom_call_target="tpu_custom_call" | custom-call | tf_op jit(solution)/shard_map/pallas_call | solution.py:368
  96.0 0.0 copy-start
  96.0 2.4 %copy.7 = bf16[4,64,2048]{2,1,0:T(8,128)(2,1)} copy(bf16[4,64,2048]{2,1,0:T(8,128)(2,1)} %get-tuple-element.8) | data formatting | bytes 2097152
  98.3 0.0 copy-done
  98.3 0.8 copy.8
Async XLA Ops:
  96.0 2.4 %copy-start = (f32[9,64,256]{2,1,0:T(8,128)S(1)}, f32[9,64,256]{2,1,0:T(8,128)}, u32[]{:S(2)}) copy-start(f32[9,64,256]{2,1,0:T(8,128)} %get-tuple-element.5) | copy-start | bytes 1769476
